TPU v7x, 512 devices: a whole 4x8x8 slice. The times are simulated.
512 devices in a mesh: ctx: 32 (over z, x), head: 16 (over y, core).
Axes of the slice: x: 4, y: 8, z: 8, core: 2. Of those that a mesh axis runs over, the one named last changes fastest.
Arguments:
- queries: bfloat16 [16384, 4096], P(('ctx', 'head')), may hold values from -64 to 64
- keys: bfloat16 [16384, 4096], P(('ctx', 'head')), may hold values from -8 to 8
- values: bfloat16 [16384, 4096], P(('ctx', 'head')), may hold values from -6 to 6
Outputs:
- attended: bfloat16 [16384, 4096], P(('ctx', 'head'))
All inputs are finite; a program needn't handle non-finite values.
Results may differ from a plain program's by a relative error of at most 0.0045.
Values may be sent and summed in bfloat16 or wider, within the bound.
No kernel may reach another device: no remote copies, remote signals or barrier semaphores. Data moves between devices by JAX's collectives and lax.ppermute only.
A program may use at most 64 MiB of HBM per device.

v0:
```python
import jax
import jax.numpy as jnp
from jax import lax
from jax.sharding import PartitionSpec as P

HEAD_SIZE = 128
BLOCK = 256
SUM = 16
BAND_REACH = 1024


def from_behind(value, axis, steps):
    count = lax.axis_size(axis)
    initial, last = (max(0, -steps), min(count, count - steps))
    return lax.ppermute(value, axis, [(source, source + steps) for source in range(initial, last)])


def summary_positions(count):
    ridx = jnp.arange(count, dtype=jnp.int32)
    return ridx // SUM * BLOCK + BLOCK - SUM + ridx % SUM


def band_scores(qblk, kb, qpos, bpos):
    scores = jnp.einsum(
        "qhd,khd->hqk", qblk, kb, preferred_element_type=jnp.float32
    ) * HEAD_SIZE ** (-0.5)
    diff = qpos[:, None] - bpos[None, :]
    band_ok = (bpos[None, :] >= 0) & (diff >= 0) & (diff < BAND_REACH)
    return (jnp.where(band_ok[None], scores, -1e30), band_ok)


def sum_scores(qblk, ks, qpos, spos):
    scores = jnp.einsum(
        "qhd,khd->hqk", qblk, ks, preferred_element_type=jnp.float32
    ) * HEAD_SIZE ** (-0.5)
    sum_ok = qpos[:, None] - spos[None, :] >= BAND_REACH
    return (jnp.where(sum_ok[None], scores, -1e30), sum_ok)


def local(queries, keys, values):
    q_dev, k_dev, v_dev = (
        lax.all_to_all(queries, "head", split_axis=1, concat_axis=0, tiled=True),
        lax.all_to_all(keys, "head", split_axis=1, concat_axis=0, tiled=True),
        lax.all_to_all(values, "head", split_axis=1, concat_axis=0, tiled=True),
    )
    tok_rows = q_dev.shape[0]
    heads_here = q_dev.shape[1] // HEAD_SIZE
    q_all = q_dev.reshape(tok_rows, heads_here, HEAD_SIZE)
    k_all = k_dev.reshape(tok_rows, heads_here, HEAD_SIZE)
    value_rows_all = v_dev.reshape(tok_rows, heads_here, HEAD_SIZE)
    base = lax.axis_index("ctx") * tok_rows
    reach_devs = (BAND_REACH + tok_rows - 1) // tok_rows
    band_k_parts = []
    band_v_parts = []
    for dist in range(reach_devs, 0, -1):
        prev_k, prev_v = from_behind((k_all, value_rows_all), "ctx", dist)
        band_k_parts.append(prev_k)
        band_v_parts.append(prev_v)
    k_band = jnp.concatenate(band_k_parts + [k_all], axis=0)
    v_band = jnp.concatenate(band_v_parts + [value_rows_all], axis=0)
    k_sum = k_all.reshape(tok_rows // BLOCK, BLOCK, heads_here, HEAD_SIZE)[
        :, BLOCK - SUM :
    ].reshape(-1, heads_here, HEAD_SIZE)
    v_sum = value_rows_all.reshape(tok_rows // BLOCK, BLOCK, heads_here, HEAD_SIZE)[
        :, BLOCK - SUM :
    ].reshape(-1, heads_here, HEAD_SIZE)
    query_rows = min(512, tok_rows)
    k_seen, v_seen = (
        lax.all_gather(k_sum, "ctx", axis=0, tiled=True),
        lax.all_gather(v_sum, "ctx", axis=0, tiled=True),
    )
    spos = summary_positions(k_seen.shape[0])
    qpos = base + 0 + jnp.arange(query_rows, dtype=jnp.int32)
    bpos = base + 0 - BAND_REACH + jnp.arange(BAND_REACH + query_rows, dtype=jnp.int32)
    sb, band_ok = band_scores(q_all, k_band, qpos, bpos)
    ss, sum_ok = sum_scores(q_all, k_seen, qpos, spos)
    top = jnp.maximum(jnp.max(sb, axis=-1), jnp.max(ss, axis=-1))
    pb = jnp.where(band_ok[None], jnp.exp(sb - top[..., None]), 0.0)
    ps = jnp.where(sum_ok[None], jnp.exp(ss - top[..., None]), 0.0)
    total = jnp.sum(pb, axis=-1) + jnp.sum(ps, axis=-1)
    numer = jnp.einsum(
        "hqk,khd->hqd", pb.astype(jnp.bfloat16), v_band, preferred_element_type=jnp.float32
    )
    numer = numer + jnp.einsum(
        "hqk,khd->hqd", ps.astype(jnp.bfloat16), v_seen, preferred_element_type=jnp.float32
    )
    outputs = (numer / total[..., None]).astype(jnp.bfloat16)
    local_out = jnp.transpose(outputs, (1, 0, 2)).reshape(tok_rows, heads_here * HEAD_SIZE)
    return lax.all_to_all(local_out, "head", split_axis=0, concat_axis=1, tiled=True)


def solution(mesh):
    placed = (P(("ctx", "head"), None), P(("ctx", "head"), None), P(("ctx", "head"), None))
    return jax.shard_map(
        local, mesh=mesh, in_specs=placed, out_specs=P(("ctx", "head"), None), check_vma=False
    )
```

profile of v0, /device:TPU:1, one launch (start us, length us, event | category | flops | bytes accessed | tf_op | source)
XLA Modules:
  0.0 202.9 jit_solution(5113818668140750158)
XLA Ops:
  0.0 1.7 copy.54
  1.7 10.2 %all-to-all-start = ((bf16[32,16,256]{2,0,1:T(8,128)(2,1)}), bf16[32,16,256]{2,0,1:T(8,128)(2,1)S(1)}, u32[]{:S(2)}, u32[]{:S(2)}) async-start(bf16[32,16,256]{2,0,1:T(8,128)(2,1)} %bitcast.48), calls=%async_computation | async-start | bytes 524288 | tf_op jit(solution)/shard_map/all_to_all | solution.py:43
  11.9 1.7 copy.52
  13.5 10.2 %all-to-all-done = bf16[32,16,256]{2,0,1:T(8,128)(2,1)S(1)} async-done(((bf16[32,16,256]{2,0,1:T(8,128)(2,1)}), bf16[32,16,256]{2,0,1:T(8,128)(2,1)S(1)}, u32[]{:S(2)}, u32[]{:S(2)}) %all-to-all-start) | async-done | bytes 262176 | tf_op jit(solution)/shard_map/all_to_all | solution.py:43
  23.7 3.4 %all-to-all-start.2 = ((bf16[32,16,256]{2,0,1:T(8,128)(2,1)}), bf16[32,16,256]{2,0,1:T(8,128)(2,1)S(1)}, u32[]{:S(2)}, u32[]{:S(2)}) async-start(bf16[32,16,256]{2,0,1:T(8,128)(2,1)} %bitcast.46), calls=%async_computation.2 | async-start | bytes 524288 | tf_op jit(solution)/shard_map/all_to_all | solution.py:44
  27.2 1.7 copy.53
  28.9 0.4 subtract_compare_fusion.2
  29.3 8.9 %all-to-all-done.2 = bf16[32,16,256]{2,0,1:T(8,128)(2,1)S(1)} async-done(((bf16[32,16,256]{2,0,1:T(8,128)(2,1)}), bf16[32,16,256]{2,0,1:T(8,128)(2,1)S(1)}, u32[]{:S(2)}, u32[]{:S(2)}) %all-to-all-start.2) | async-done | bytes 262176 | tf_op jit(solution)/shard_map/all_to_all | solution.py:44
  38.2 3.4 %all-to-all-start.1 = ((bf16[32,16,256]{2,0,1:T(8,128)(2,1)}), bf16[32,16,256]{2,0,1:T(8,128)(2,1)S(1)}, u32[]{:S(2)}, u32[]{:S(2)}) async-start(bf16[32,16,256]{2,0,1:T(8,128)(2,1)} %bitcast.47), calls=%async_computation.1 | async-start | bytes 524288 | tf_op jit(solution)/shard_map/all_to_all | solution.py:42
  41.6 1.3 fusion.7
  43.0 3.7 %collective-permute-start = (bf16[512,2,128]{2,0,1:T(8,128)(2,1)S(1)}, bf16[512,2,128]{2,0,1:T(8,128)(2,1)}, u32[]{:S(2)}, u32[]{:S(2)}) collective-permute-start(bf16[512,2,128]{2,0,1:T(8,128)(2,1)S(1)} %copy.21), channel_id=1, source_target_pairs={{0,32},{16,48},{32,64},{48,80},{64,96},{80,112},{96,128},{112,144}... | collective-permute-start | bytes 786440 | tf_op jit(solution)/shard_map/ppermute | solution.py:15
  46.7 2.9 %collective-permute-start.1 = (bf16[512,2,128]{2,0,1:T(8,128)(2,1)S(1)}, bf16[512,2,128]{2,0,1:T(8,128)(2,1)}, u32[]{:S(2)}, u32[]{:S(2)}) collective-permute-start(bf16[512,2,128]{2,0,1:T(8,128)(2,1)S(1)} %copy.21), channel_id=1, source_target_pairs={{0,16},{16,32},{32,48},{48,64},{64,80},{80,96},{96,112},{112,128},... | collective-permute-start | bytes 786440 | tf_op jit(solution)/shard_map/ppermute | solution.py:15
  49.9 4.8 %collective-permute-start.2 = (bf16[512,2,128]{2,0,1:T(8,128)(2,1)S(1)}, bf16[512,2,128]{2,0,1:T(8,128)(2,1)}, u32[]{:S(2)}, u32[]{:S(2)}) collective-permute-start(bf16[512,2,128]{2,0,1:T(8,128)(2,1)S(1)} %copy.29), channel_id=1, source_target_pairs={{0,32},{16,48},{32,64},{48,80},{64,96},{80,112},{96,128},{112,144}... | collective-permute-start | bytes 786440 | tf_op jit(solution)/shard_map/ppermute | solution.py:15
  54.7 3.8 %collective-permute-start.3 = (bf16[512,2,128]{2,0,1:T(8,128)(2,1)S(1)}, bf16[512,2,128]{2,0,1:T(8,128)(2,1)}, u32[]{:S(2)}, u32[]{:S(2)}) collective-permute-start(bf16[512,2,128]{2,0,1:T(8,128)(2,1)S(1)} %copy.29), channel_id=1, source_target_pairs={{0,16},{16,32},{32,48},{48,64},{64,80},{80,96},{96,112},{112,128},... | collective-permute-start | bytes 786440 | tf_op jit(solution)/shard_map/ppermute | solution.py:15
  58.6 52.4 %all_gather.6 = bf16[1024,2,128]{2,0,1:T(8,128)(2,1)S(1)} all-gather(bf16[32,2,128]{2,0,1:T(8,128)(2,1)S(1)} %bitcast.58), channel_id=1, replica_groups=mesh['ctx'=32,'head'=16] {'ctx'}, dimensions={0}, use_global_device_ids=true | all-gather | bytes 540672 | tf_op jit(solution)/shard_map/all_gather | solution.py:69
  111.1 37.2 %all_gather.7 = bf16[1024,2,128]{2,0,1:T(8,128)(2,1)S(1)} all-gather(bf16[32,2,128]{2,0,1:T(8,128)(2,1)S(1)} %bitcast.59), channel_id=1, replica_groups=mesh['ctx'=32,'head'=16] {'ctx'}, dimensions={0}, use_global_device_ids=true | all-gather | bytes 540672 | tf_op jit(solution)/shard_map/all_gather | solution.py:70
  148.2 1.1 fusion.3
  149.3 2.4 %fusion = (f32[2,512]{1,0:T(2,128)S(1)}, f32[2,1536,512]{2,1,0:T(8,128)S(1)}) fusion(pred[512,1536]{0,1:T(8,128)(4,1)S(1)} %fusion.7, bf16[512,2,128]{2,1,0:T(2,128)(2,1)S(1)} %reshape.153, bf16[512,2,128]{2,0,1:T(8,128)(2,1)S(1)} %copy.21, bf16[512,2,128]{2,0,1:T(8,128)(2,1)} %collective-permute-done.1, bf16[512,2,128]{2,0,1:T(8,128)(2,1)} %collective-permute-done), kind=kOutput, calls=%fused_computation.2 | convolution fusion | flops 409730048 | bytes 8130560 | tf_op jit(solution)/shard_map/qhd,khd->hqk/dot_general | solution.py:24
  151.8 1.7 fusion.1
  153.4 1.6 fusion.11
  155.0 1.5 fusion.9
  156.6 3.6 %fusion.23 = bf16[512,2,128]{2,0,1:T(8,128)(2,1)S(1)} fusion(f32[2,512,128]{2,1,0:T(8,128)S(1)} %fusion.11, f32[2,1536,512]{2,1,0:T(8,128)S(1)} %get-tuple-element.6, f32[2,512]{1,0:T(2,128)S(1)} %max.7, pred[512,1536]{0,1:T(8,128)(4,1)S(1)} %fusion.7, bf16[512,2,128]{2,0,1:T(8,128)(2,1)S(1)} %copy.29, bf16[512,2,128]{2,0,1:T(8,128)(2,1)} %collective-permute-done.3, ...), kind=kOutput, calls=%fused_computation.22 | convolution fusion | flops 413270016 | bytes 8658944 | tf_op jit(solution)/shard_map/hqk,khd->hqd/dot_general | solution.py:81
  160.6 41.6 %all_to_all.67 = bf16[16,32,256]{2,1,0:T(8,128)(2,1)S(1)} all-to-all(bf16[16,32,256]{2,1,0:T(8,128)(2,1)S(1)} %all_to_all.59), channel_id=1, replica_groups=mesh['ctx'=32,'head'=16] {'head'}, dimensions={0} | all-to-all | bytes 524288 | tf_op jit(solution)/shard_map/all_to_all | solution.py:89
  202.2 0.7 copy.40
  (24 shorter events, 0.9 us)
Async XLA Ops:
  1.7 22.1 %all-to-all-start = ((bf16[32,16,256]{2,0,1:T(8,128)(2,1)}), bf16[32,16,256]{2,0,1:T(8,128)(2,1)S(1)}, u32[]{:S(2)}, u32[]{:S(2)}) async-start(bf16[32,16,256]{2,0,1:T(8,128)(2,1)} %bitcast.48), calls=%async_computation | async-start | bytes 524288 | tf_op jit(solution)/shard_map/all_to_all | solution.py:43
  23.7 14.5 %all-to-all-start.2 = ((bf16[32,16,256]{2,0,1:T(8,128)(2,1)}), bf16[32,16,256]{2,0,1:T(8,128)(2,1)S(1)}, u32[]{:S(2)}, u32[]{:S(2)}) async-start(bf16[32,16,256]{2,0,1:T(8,128)(2,1)} %bitcast.46), calls=%async_computation.2 | async-start | bytes 524288 | tf_op jit(solution)/shard_map/all_to_all | solution.py:44
  38.2 20.3 %all-to-all-start.1 = ((bf16[32,16,256]{2,0,1:T(8,128)(2,1)}), bf16[32,16,256]{2,0,1:T(8,128)(2,1)S(1)}, u32[]{:S(2)}, u32[]{:S(2)}) async-start(bf16[32,16,256]{2,0,1:T(8,128)(2,1)} %bitcast.47), calls=%async_computation.1 | async-start | bytes 524288 | tf_op jit(solution)/shard_map/all_to_all | solution.py:42
  43.0 106.3 %collective-permute-start = (bf16[512,2,128]{2,0,1:T(8,128)(2,1)S(1)}, bf16[512,2,128]{2,0,1:T(8,128)(2,1)}, u32[]{:S(2)}, u32[]{:S(2)}) collective-permute-start(bf16[512,2,128]{2,0,1:T(8,128)(2,1)S(1)} %copy.21), channel_id=1, source_target_pairs={{0,32},{16,48},{32,64},{48,80},{64,96},{80,112},{96,128},{112,144}... | collective-permute-start | bytes 786440 | tf_op jit(solution)/shard_map/ppermute | solution.py:15
  46.7 102.6 %collective-permute-start.1 = (bf16[512,2,128]{2,0,1:T(8,128)(2,1)S(1)}, bf16[512,2,128]{2,0,1:T(8,128)(2,1)}, u32[]{:S(2)}, u32[]{:S(2)}) collective-permute-start(bf16[512,2,128]{2,0,1:T(8,128)(2,1)S(1)} %copy.21), channel_id=1, source_target_pairs={{0,16},{16,32},{32,48},{48,64},{64,80},{80,96},{96,112},{112,128},... | collective-permute-start | bytes 786440 | tf_op jit(solution)/shard_map/ppermute | solution.py:15
  49.9 106.6 %collective-permute-start.2 = (bf16[512,2,128]{2,0,1:T(8,128)(2,1)S(1)}, bf16[512,2,128]{2,0,1:T(8,128)(2,1)}, u32[]{:S(2)}, u32[]{:S(2)}) collective-permute-start(bf16[512,2,128]{2,0,1:T(8,128)(2,1)S(1)} %copy.29), channel_id=1, source_target_pairs={{0,32},{16,48},{32,64},{48,80},{64,96},{80,112},{96,128},{112,144}... | collective-permute-start | bytes 786440 | tf_op jit(solution)/shard_map/ppermute | solution.py:15
  54.7 101.9 %collective-permute-start.3 = (bf16[512,2,128]{2,0,1:T(8,128)(2,1)S(1)}, bf16[512,2,128]{2,0,1:T(8,128)(2,1)}, u32[]{:S(2)}, u32[]{:S(2)}) collective-permute-start(bf16[512,2,128]{2,0,1:T(8,128)(2,1)S(1)} %copy.29), channel_id=1, source_target_pairs={{0,16},{16,32},{32,48},{48,64},{64,80},{80,96},{96,112},{112,128},... | collective-permute-start | bytes 786440 | tf_op jit(solution)/shard_map/ppermute | solution.py:15
where the time goes:
time: 204 us; the launch traced here: 203 us
  blocking collectives  131 us (64%)
  starting transfers between devices  32.3 us (16%)
  waiting for transfers between devices  19.1 us (9%)
  matrix products  8.69 us (4%)
  local copies, waits for them, and re-layouts  6.62 us (3%)
  other arithmetic  4.88 us (2%)
    all_gather x1, blocking collectives, local(): lax.all_gather(k_sum, 'ctx', axis=0, tiled=True)  52.4 us
    all_to_all x1, blocking collectives, local(): lax.all_to_all(local_out, 'head', split_axis=0, concat_axis=1, tiled=True)  41.6 us
    all_gather x1, blocking collectives, local(): lax.all_gather(v_sum, 'ctx', axis=0, tiled=True)  37.2 us
    ppermute x4, starting transfers between devices, from_behind(): lax.ppermute(value, axis, [(source, source + steps) for source in range(i...  15.3 us
    all_to_all x1, starting transfers between devices, local(): lax.all_to_all(keys, 'head', split_axis=1, concat_axis=0, tiled=True)  10.2 us
    all_to_all x1, waiting for transfers between devices, local(): lax.all_to_all(keys, 'head', split_axis=1, concat_axis=0, tiled=True)  10.2 us
    all_to_all x1, waiting for transfers between devices, local(): lax.all_to_all(values, 'head', split_axis=1, concat_axis=0, tiled=True)  8.91 us
  transfers between devices with their start and end apart: 7, of which 2 were waited for; matrix products, arithmetic and copies ran while one was open for 7% of the time, Pallas kernels for 0%

commit v1 on v0

--- a/solution.py
+++ b/solution.py
@@ -7,6 +7,13 @@
 BLOCK = 256
 SUM = 16
 BAND_REACH = 1024
+
+
+def exchange_gather(value, name, dim):
+    devices = lax.axis_size(name)
+    blocks = jnp.stack([value for _ in range(devices)])
+    blocks = lax.all_to_all(blocks, name, split_axis=0, concat_axis=0)
+    return jnp.concatenate(blocks, axis=dim)
 
 
 def from_behind(value, axis, steps):
@@ -67,7 +74,7 @@
     query_rows = min(512, tok_rows)
     k_seen, v_seen = (
         lax.all_gather(k_sum, "ctx", axis=0, tiled=True),
-        lax.all_gather(v_sum, "ctx", axis=0, tiled=True),
+        exchange_gather(v_sum, "ctx", 0),
     )
     spos = summary_positions(k_seen.shape[0])
     qpos = base + 0 + jnp.arange(query_rows, dtype=jnp.int32)

time: 204 us -> 171 us (0.84)
  blocking collectives: 131 us -> 84.1 us
  starting transfers between devices: 32.3 us -> 37.7 us
  waiting for transfers between devices: 19.1 us -> 24.5 us
  matrix products: 8.69 us -> 10.9 us
    all_gather x1 -> x0, blocking collectives: 37.2 us -> none  [local(): lax.all_gather(v_sum, 'ctx', axis=0, tiled=True)]
    all_to_all x1, blocking collectives: 41.6 us -> 31.7 us  [local(): lax.all_to_all(local_out, 'head', split_axis=0, concat_axis=1, tiled=True)]
    all_to_all x0 -> x1, starting transfers between devices: none -> 5.41 us  [exchange_gather(): blocks = lax.all_to_all(blocks, name, split_axis=0, concat_axis=0)]
    all_to_all x0 -> x1, waiting for transfers between devices: none -> 5.35 us  [exchange_gather(): blocks = lax.all_to_all(blocks, name, split_axis=0, concat_axis=0)]
  transfers between devices with their start and end apart: 7 -> 8, of which waited for: 2 -> 3; matrix products, arithmetic and copies ran while one was open for 7% -> 10% of each run, Pallas kernels for 0% -> 0%
where the time goes in v1:
time: 171 us; the launch traced here: 170 us
  blocking collectives  84.1 us (49%)
  starting transfers between devices  37.7 us (22%)
  waiting for transfers between devices  24.5 us (14%)
  matrix products  10.9 us (6%)
  local copies, waits for them, and re-layouts  8.19 us (5%)
  other arithmetic  4.85 us (3%)
    all_gather x1, blocking collectives, local(): lax.all_gather(k_sum, 'ctx', axis=0, tiled=True)  52.4 us
    all_to_all x1, blocking collectives, local(): lax.all_to_all(local_out, 'head', split_axis=0, concat_axis=1, tiled=True)  31.7 us
    ppermute x4, starting transfers between devices, from_behind(): lax.ppermute(value, axis, [(source, source + steps) for source in range(i...  15.2 us
    all_to_all x1, starting transfers between devices, local(): lax.all_to_all(keys, 'head', split_axis=1, concat_axis=0, tiled=True)  10.2 us
    all_to_all x1, waiting for transfers between devices, local(): lax.all_to_all(keys, 'head', split_axis=1, concat_axis=0, tiled=True)  10.2 us
    all_to_all x1, waiting for transfers between devices, local(): lax.all_to_all(values, 'head', split_axis=1, concat_axis=0, tiled=True)  8.91 us
    all_to_all x1, starting transfers between devices, exchange_gather(): blocks = lax.all_to_all(blocks, name, split_axis=0, concat_axis=0)  5.41 us
    all_to_all x1, waiting for transfers between devices, exchange_gather(): blocks = lax.all_to_all(blocks, name, split_axis=0, concat_axis=0)  5.35 us
  transfers between devices with their start and end apart: 8, of which 3 were waited for; matrix products, arithmetic and copies ran while one was open for 10% of the time, Pallas kernels for 0%

profile of v1, /device:TPU:1, one launch (start us, length us, event | category | flops | bytes accessed | tf_op | source)
XLA Modules:
  0.0 170.4 jit_solution(15636296580716383020)
XLA Ops:
  0.0 1.7 copy.71
  1.7 10.2 %all-to-all-start = ((bf16[32,16,256]{2,0,1:T(8,128)(2,1)}), bf16[32,16,256]{2,0,1:T(8,128)(2,1)S(1)}, u32[]{:S(2)}, u32[]{:S(2)}) async-start(bf16[32,16,256]{2,0,1:T(8,128)(2,1)} %bitcast.49), calls=%async_computation | async-start | bytes 524288 | tf_op jit(solution)/shard_map/all_to_all | solution.py:50
  11.9 1.7 copy.69
  13.6 10.2 %all-to-all-done = bf16[32,16,256]{2,0,1:T(8,128)(2,1)S(1)} async-done(((bf16[32,16,256]{2,0,1:T(8,128)(2,1)}), bf16[32,16,256]{2,0,1:T(8,128)(2,1)S(1)}, u32[]{:S(2)}, u32[]{:S(2)}) %all-to-all-start) | async-done | bytes 262176 | tf_op jit(solution)/shard_map/all_to_all | solution.py:50
  23.7 3.4 %all-to-all-start.2 = ((bf16[32,16,256]{2,0,1:T(8,128)(2,1)}), bf16[32,16,256]{2,0,1:T(8,128)(2,1)S(1)}, u32[]{:S(2)}, u32[]{:S(2)}) async-start(bf16[32,16,256]{2,0,1:T(8,128)(2,1)} %bitcast.47), calls=%async_computation.2 | async-start | bytes 524288 | tf_op jit(solution)/shard_map/all_to_all | solution.py:51
  27.2 1.7 copy.70
  29.3 8.9 %all-to-all-done.2 = bf16[32,16,256]{2,0,1:T(8,128)(2,1)S(1)} async-done(((bf16[32,16,256]{2,0,1:T(8,128)(2,1)}), bf16[32,16,256]{2,0,1:T(8,128)(2,1)S(1)}, u32[]{:S(2)}, u32[]{:S(2)}) %all-to-all-start.2) | async-done | bytes 262176 | tf_op jit(solution)/shard_map/all_to_all | solution.py:51
  38.2 3.4 %all-to-all-start.1 = ((bf16[32,16,256]{2,0,1:T(8,128)(2,1)}), bf16[32,16,256]{2,0,1:T(8,128)(2,1)S(1)}, u32[]{:S(2)}, u32[]{:S(2)}) async-start(bf16[32,16,256]{2,0,1:T(8,128)(2,1)} %bitcast.48), calls=%async_computation.1 | async-start | bytes 524288 | tf_op jit(solution)/shard_map/all_to_all | solution.py:49
  41.6 1.3 fusion.7
  43.0 3.7 %collective-permute-start = (bf16[512,2,128]{2,0,1:T(8,128)(2,1)S(1)}, bf16[512,2,128]{2,0,1:T(8,128)(2,1)}, u32[]{:S(2)}, u32[]{:S(2)}) collective-permute-start(bf16[512,2,128]{2,0,1:T(8,128)(2,1)S(1)} %copy.37), channel_id=1, source_target_pairs={{0,32},{16,48},{32,64},{48,80},{64,96},{80,112},{96,128},{112,144}... | collective-permute-start | bytes 786440 | tf_op jit(solution)/shard_map/ppermute | solution.py:22
  46.7 2.9 %collective-permute-start.1 = (bf16[512,2,128]{2,0,1:T(8,128)(2,1)S(1)}, bf16[512,2,128]{2,0,1:T(8,128)(2,1)}, u32[]{:S(2)}, u32[]{:S(2)}) collective-permute-start(bf16[512,2,128]{2,0,1:T(8,128)(2,1)S(1)} %copy.37), channel_id=1, source_target_pairs={{0,16},{16,32},{32,48},{48,64},{64,80},{80,96},{96,112},{112,128},... | collective-permute-start | bytes 786440 | tf_op jit(solution)/shard_map/ppermute | solution.py:22
  49.9 4.8 %collective-permute-start.2 = (bf16[512,2,128]{2,0,1:T(8,128)(2,1)S(1)}, bf16[512,2,128]{2,0,1:T(8,128)(2,1)}, u32[]{:S(2)}, u32[]{:S(2)}) collective-permute-start(bf16[512,2,128]{2,0,1:T(8,128)(2,1)S(1)} %copy.45), channel_id=1, source_target_pairs={{0,32},{16,48},{32,64},{48,80},{64,96},{80,112},{96,128},{112,144}... | collective-permute-start | bytes 786440 | tf_op jit(solution)/shard_map/ppermute | solution.py:22
  54.7 3.8 %collective-permute-start.3 = (bf16[512,2,128]{2,0,1:T(8,128)(2,1)S(1)}, bf16[512,2,128]{2,0,1:T(8,128)(2,1)}, u32[]{:S(2)}, u32[]{:S(2)}) collective-permute-start(bf16[512,2,128]{2,0,1:T(8,128)(2,1)S(1)} %copy.45), channel_id=1, source_target_pairs={{0,16},{16,32},{32,48},{48,64},{64,80},{80,96},{96,112},{112,128},... | collective-permute-start | bytes 786440 | tf_op jit(solution)/shard_map/ppermute | solution.py:22
  58.6 52.4 %all_gather.3 = bf16[1024,2,128]{2,0,1:T(8,128)(2,1)S(1)} all-gather(bf16[32,2,128]{2,0,1:T(8,128)(2,1)S(1)} %bitcast.60), channel_id=1, replica_groups=mesh['ctx'=32,'head'=16] {'ctx'}, dimensions={0}, use_global_device_ids=true | all-gather | bytes 540672 | tf_op jit(solution)/shard_map/all_gather | solution.py:76
  111.1 0.9 stack.3
  112.0 5.4 %all-to-all-start.3 = ((bf16[32,32,2,128]{3,1,2,0:T(8,128)(2,1)}), bf16[32,32,2,128]{3,1,2,0:T(8,128)(2,1)S(1)}, u32[]{:S(2)}, u32[]{:S(2)}) async-start(bf16[32,32,2,128]{3,1,2,0:T(8,128)(2,1)} %stack.3), calls=%async_computation.3 | async-start | bytes 1048576 | tf_op jit(solution)/shard_map/all_to_all | solution.py:15
  117.4 1.1 fusion.3
  118.5 2.8 %fusion = (f32[2,512]{1,0:T(2,128)S(1)}, f32[2,1536,512]{2,1,0:T(8,128)S(1)}) fusion(pred[512,1536]{0,1:T(8,128)(4,1)S(1)} %fusion.7, bf16[512,2,128]{2,1,0:T(2,128)(2,1)S(1)} %reshape.155, bf16[512,2,128]{2,0,1:T(8,128)(2,1)S(1)} %copy.37, bf16[512,2,128]{2,0,1:T(8,128)(2,1)} %collective-permute-done.1, bf16[512,2,128]{2,0,1:T(8,128)(2,1)} %collective-permute-done), kind=kOutput, calls=%fused_computation.2 | convolution fusion | flops 409730048 | bytes 8130560 | tf_op jit(solution)/shard_map/qhd,khd->hqk/dot_general | solution.py:31
  121.4 1.5 fusion.9
  122.8 1.7 fusion.1
  124.6 5.3 %all-to-all-done.3 = bf16[32,32,2,128]{3,1,2,0:T(8,128)(2,1)S(1)} async-done(((bf16[32,32,2,128]{3,1,2,0:T(8,128)(2,1)}), bf16[32,32,2,128]{3,1,2,0:T(8,128)(2,1)S(1)}, u32[]{:S(2)}, u32[]{:S(2)}) %all-to-all-start.3) | async-done | bytes 524320 | tf_op jit(solution)/shard_map/all_to_all | solution.py:15
  130.0 3.4 %fusion.11 = f32[2,512,128]{2,1,0:T(8,128)S(1)} fusion(bf16[1024,2,128]{2,0,1:T(8,128)(2,1)S(1)} %bitcast.56, f32[2,512,1024]{2,1,0:T(8,128)} %copy-done.2, f32[2,512]{1,0:T(2,128)S(1)} %max.7, pred[512,1024]{1,0:T(8,128)(4,1)S(1)} %subtract_compare_fusion.2), kind=kOutput, calls=%fused_computation.17 | convolution fusion | flops 273678336 | bytes 5771264 | tf_op jit(solution)/shard_map/hqk,khd->hqd/dot_general | solution.py:91
  134.0 3.6 %fusion.23 = bf16[512,2,128]{2,0,1:T(8,128)(2,1)S(1)} fusion(f32[2,512,128]{2,1,0:T(8,128)S(1)} %fusion.11, f32[2,1536,512]{2,1,0:T(8,128)S(1)} %copy-done.1, f32[2,512]{1,0:T(2,128)S(1)} %max.7, pred[512,1536]{0,1:T(8,128)(4,1)S(1)} %fusion.7, bf16[512,2,128]{2,0,1:T(8,128)(2,1)S(1)} %copy.45, bf16[512,2,128]{2,0,1:T(8,128)(2,1)} %collective-permute-done.3, ...), kind=kOutput, calls=%fused_computation.22 | convolution fusion | flops 413270016 | bytes 8658944 | tf_op jit(solution)/shard_map/hqk,khd->hqd/dot_general | solution.py:88
  138.0 31.7 %all_to_all.72 = bf16[16,32,256]{2,1,0:T(8,128)(2,1)S(1)} all-to-all(bf16[16,32,256]{2,1,0:T(8,128)(2,1)S(1)} %all_to_all.63), channel_id=1, replica_groups=mesh['ctx'=32,'head'=16] {'head'}, dimensions={0} | all-to-all | bytes 524288 | tf_op jit(solution)/shard_map/all_to_all | solution.py:96
  (33 shorter events, 2.7 us)
Async XLA Ops:
  1.7 22.1 %all-to-all-start = ((bf16[32,16,256]{2,0,1:T(8,128)(2,1)}), bf16[32,16,256]{2,0,1:T(8,128)(2,1)S(1)}, u32[]{:S(2)}, u32[]{:S(2)}) async-start(bf16[32,16,256]{2,0,1:T(8,128)(2,1)} %bitcast.49), calls=%async_computation | async-start | bytes 524288 | tf_op jit(solution)/shard_map/all_to_all | solution.py:50
  23.7 14.5 %all-to-all-start.2 = ((bf16[32,16,256]{2,0,1:T(8,128)(2,1)}), bf16[32,16,256]{2,0,1:T(8,128)(2,1)S(1)}, u32[]{:S(2)}, u32[]{:S(2)}) async-start(bf16[32,16,256]{2,0,1:T(8,128)(2,1)} %bitcast.47), calls=%async_computation.2 | async-start | bytes 524288 | tf_op jit(solution)/shard_map/all_to_all | solution.py:51
  38.2 20.3 %all-to-all-start.1 = ((bf16[32,16,256]{2,0,1:T(8,128)(2,1)}), bf16[32,16,256]{2,0,1:T(8,128)(2,1)S(1)}, u32[]{:S(2)}, u32[]{:S(2)}) async-start(bf16[32,16,256]{2,0,1:T(8,128)(2,1)} %bitcast.48), calls=%async_computation.1 | async-start | bytes 524288 | tf_op jit(solution)/shard_map/all_to_all | solution.py:49
  43.0 75.5 %collective-permute-start = (bf16[512,2,128]{2,0,1:T(8,128)(2,1)S(1)}, bf16[512,2,128]{2,0,1:T(8,128)(2,1)}, u32[]{:S(2)}, u32[]{:S(2)}) collective-permute-start(bf16[512,2,128]{2,0,1:T(8,128)(2,1)S(1)} %copy.37), channel_id=1, source_target_pairs={{0,32},{16,48},{32,64},{48,80},{64,96},{80,112},{96,128},{112,144}... | collective-permute-start | bytes 786440 | tf_op jit(solution)/shard_map/ppermute | solution.py:22
  46.7 71.8 %collective-permute-start.1 = (bf16[512,2,128]{2,0,1:T(8,128)(2,1)S(1)}, bf16[512,2,128]{2,0,1:T(8,128)(2,1)}, u32[]{:S(2)}, u32[]{:S(2)}) collective-permute-start(bf16[512,2,128]{2,0,1:T(8,128)(2,1)S(1)} %copy.37), channel_id=1, source_target_pairs={{0,16},{16,32},{32,48},{48,64},{64,80},{80,96},{96,112},{112,128},... | collective-permute-start | bytes 786440 | tf_op jit(solution)/shard_map/ppermute | solution.py:22
  49.9 83.5 %collective-permute-start.2 = (bf16[512,2,128]{2,0,1:T(8,128)(2,1)S(1)}, bf16[512,2,128]{2,0,1:T(8,128)(2,1)}, u32[]{:S(2)}, u32[]{:S(2)}) collective-permute-start(bf16[512,2,128]{2,0,1:T(8,128)(2,1)S(1)} %copy.45), channel_id=1, source_target_pairs={{0,32},{16,48},{32,64},{48,80},{64,96},{80,112},{96,128},{112,144}... | collective-permute-start | bytes 786440 | tf_op jit(solution)/shard_map/ppermute | solution.py:22
  54.7 78.7 %collective-permute-start.3 = (bf16[512,2,128]{2,0,1:T(8,128)(2,1)S(1)}, bf16[512,2,128]{2,0,1:T(8,128)(2,1)}, u32[]{:S(2)}, u32[]{:S(2)}) collective-permute-start(bf16[512,2,128]{2,0,1:T(8,128)(2,1)S(1)} %copy.45), channel_id=1, source_target_pairs={{0,16},{16,32},{32,48},{48,64},{64,80},{80,96},{96,112},{112,128},... | collective-permute-start | bytes 786440 | tf_op jit(solution)/shard_map/ppermute | solution.py:22
  112.0 17.9 %all-to-all-start.3 = ((bf16[32,32,2,128]{3,1,2,0:T(8,128)(2,1)}), bf16[32,32,2,128]{3,1,2,0:T(8,128)(2,1)S(1)}, u32[]{:S(2)}, u32[]{:S(2)}) async-start(bf16[32,32,2,128]{3,1,2,0:T(8,128)(2,1)} %stack.3), calls=%async_computation.3 | async-start | bytes 1048576 | tf_op jit(solution)/shard_map/all_to_all | solution.py:15
  118.5 2.9 %copy-start.2 = (f32[2,512,1024]{2,1,0:T(8,128)}, f32[2,512,1024]{2,1,0:T(8,128)S(1)}, u32[]{:S(2)}) copy-start(f32[2,512,1024]{2,1,0:T(8,128)S(1)} %get-tuple-element.8) | copy-start | bytes 12582916
  121.3 3.2 %copy-start = (f32[2,1536,512]{2,1,0:T(8,128)}, f32[2,1536,512]{2,1,0:T(8,128)S(1)}, u32[]{:S(2)}) copy-start(f32[2,1536,512]{2,1,0:T(8,128)S(1)} %get-tuple-element.6) | copy-start | bytes 18874372
  129.9 4.0 %copy-start.1 = (f32[2,1536,512]{2,1,0:T(8,128)S(1)}, f32[2,1536,512]{2,1,0:T(8,128)}, u32[]{:S(2)}) copy-start(f32[2,1536,512]{2,1,0:T(8,128)} %copy-done) | copy-start | bytes 18874372
